TPU v7x, 256 devices: a whole 4x4x8 slice. The times are simulated.
256 devices in a mesh: edge: 64 (over y, z, core), pix: 4 (over x).
Axes of the slice: x: 4, y: 4, z: 8, core: 2. Of those that a mesh axis runs over, the one named last changes fastest.
Arguments:
- features: bfloat16 [128, 48, 64, 128], P('edge', 'pix'), may hold values from -6 to 6
- poses: float32 [128, 6], replicated, may hold values from -1.5 to 1.5
- inv_depth: float32 [128, 3072], P('edge', 'pix'), may hold values from 0.25 to 2
- hidden: bfloat16 [256, 48, 64, 128], P('edge', 'pix'), may hold values from -1 to 1
- edges: int32 [256, 2], P('edge'), may hold values from 0 to 127, as said below
- counts: int32 [64], P('edge'), may hold values from 1 to 4, 128 in all
- w_gates: bfloat16 [9, 256, 256], replicated, may hold values from -0.125 to 0.125
- w_cand: bfloat16 [9, 256, 128], replicated, may hold values from -0.125 to 0.125
- w_head: bfloat16 [4, 128], replicated, may hold values from -0.5 to 0.5
Outputs:
- hidden_out: bfloat16 [256, 48, 64, 128], P('edge', 'pix')
- pose_update: float32 [128, 6], P('edge')
- depth_update: float32 [128, 3072], P('edge', 'pix')
Inputs may be any that keep to these rules, and one draw needn't show every extreme that they name: `edges`: slot s lies on node n = s // 4; its source frame is 2n or 2n + 1 and its target is one of the frames 2n to 2n + 3 other than the source; on the last node the target is the other frame of its own pair. The first slot of node n goes from frame 2n to frame 2n + 2 (on the last node to 2n + 1). Dead slots hold such pairs too.
All inputs are finite; a program needn't handle non-finite values. No bound on the sum of `counts` on one device may be relied on, other than what follows from the above.
Results may differ from a plain program's by a relative error of at most 0.011.
Values may be sent and summed in bfloat16 or wider, within the bound.
No kernel may reach another device: no remote copies, remote signals or barrier semaphores. Data moves between devices by JAX's collectives and lax.ppermute only.
A program may use at most 192 MiB of HBM per device.

v0:
```python
import math
import jax
import jax.numpy as jnp
from jax import lax
from jax.sharding import PartitionSpec as P

PRECISE = lax.Precision.HIGHEST
POSE_DAMPING = 0.1
DEPTH_DAMPING = 0.1


def passed_along(value, axis, steps):
    count = lax.axis_size(axis)
    first, last = (max(0, -steps), min(count, count - steps))
    return lax.ppermute(value, axis, [(source, source + steps) for source in range(first, last)])


def padded_2(cells, sides, width):
    for axis, dim in sides:
        count = lax.axis_size(axis)
        ends = count - 1
        head = lax.slice_in_dim(cells, 0, width, axis=dim)
        tail = lax.slice_in_dim(cells, cells.shape[dim] - width, cells.shape[dim], axis=dim)
        cells = jnp.concatenate(
            [
                lax.ppermute(tail, axis, [(i, (i + 1) % count) for i in range(ends)]),
                cells,
                lax.ppermute(head, axis, [((i + 1) % count, i) for i in range(ends)]),
            ],
            axis=dim,
        )
    return cells


def pixel_coords(row_start, row_count, total_rows, col_count):
    row_ids = (row_start + lax.broadcasted_iota(jnp.int32, (row_count, col_count), 0)).astype(
        jnp.float32
    )
    col_ids = lax.broadcasted_iota(jnp.int32, (row_count, col_count), 1).astype(jnp.float32)
    half_width = col_count / 2.0
    horizontal = (col_ids - (col_count - 1) / 2.0) / half_width
    vertical = (row_ids - (total_rows - 1) / 2.0) / half_width
    return (horizontal.reshape(-1), vertical.reshape(-1))


def match_rows(queries, targets, factor):
    scores = jnp.einsum("pc,qc->pq", queries, targets, preferred_element_type=jnp.float32) * factor
    row_max = jnp.max(scores, axis=1, keepdims=True)
    weights = jnp.exp(scores - row_max)
    row_total = jnp.sum(weights, axis=1, keepdims=True)
    weighted_sum = jnp.dot(
        weights.astype(jnp.bfloat16), targets, preferred_element_type=jnp.float32
    )
    return (weighted_sum / row_total).astype(jnp.bfloat16)


def conv_taps(framed, weight, row_count, col_count):
    padded = jnp.pad(framed, ((0, 0), (0, 0), (1, 1), (0, 0)))
    result = None
    for tap_index in range(9):
        row_off = tap_index // 3
        col_off = tap_index % 3
        window = padded[:, row_off : row_off + row_count, col_off : col_off + col_count, :]
        tap_term = jnp.einsum(
            "srwc,cd->srwd", window, weight[tap_index], preferred_element_type=jnp.float32
        )
        result = tap_term if tap_index == 0 else result + tap_term
    return result


def bundle_terms(head_out, live_mask, inv_rho, xi_rel, src_local, tgt_local, horizontal, vertical):
    flow_pred = head_out[:, 0:2]
    confidence = jax.nn.sigmoid(head_out[:, 2:4]) * live_mask[:, None, None]
    unit_row = jnp.ones_like(inv_rho)
    zero_row = jnp.zeros_like(inv_rho)
    horiz_row = horizontal[None, :] * unit_row
    vert_row = vertical[None, :] * unit_row
    jacobian_horiz = jnp.stack(
        [
            inv_rho,
            zero_row,
            -horiz_row * inv_rho,
            -horiz_row * vert_row,
            1.0 + horiz_row * horiz_row,
            -vert_row,
        ],
        axis=1,
    )
    jacobian_vert = jnp.stack(
        [
            zero_row,
            inv_rho,
            -vert_row * inv_rho,
            -(1.0 + vert_row * vert_row),
            horiz_row * vert_row,
            horiz_row,
        ],
        axis=1,
    )
    jacobian = jnp.stack([jacobian_horiz, jacobian_vert], axis=1)
    predicted = jnp.einsum("skjp,sj->skp", jacobian, xi_rel, precision=PRECISE)
    residual = flow_pred - predicted
    forward_shift = xi_rel[:, 2:3]
    depth_jacobian = jnp.stack(
        [xi_rel[:, 0:1] - horiz_row * forward_shift, xi_rel[:, 1:2] - vert_row * forward_shift],
        axis=1,
    )
    frame_ids = jnp.arange(4, dtype=jnp.int32)
    select = (tgt_local[:, None] == frame_ids[None, :]).astype(jnp.float32) - (
        src_local[:, None] == frame_ids[None, :]
    ).astype(jnp.float32)
    slot_count, pix_count = inv_rho.shape
    pose_jacobian = (select[:, None, :, None, None] * jacobian[:, :, None, :, :]).reshape(
        slot_count, 2, 24, pix_count
    )
    weighted = pose_jacobian * confidence[:, :, None, :]
    pose_pose = jnp.einsum("skip,skjp->ij", weighted, pose_jacobian, precision=PRECISE)
    pose_rhs = jnp.einsum("skip,skp->i", weighted, residual, precision=PRECISE)
    pose_depth_slot = jnp.einsum("skip,skp->sip", weighted, depth_jacobian, precision=PRECISE)
    depth_depth_slot = jnp.sum(confidence * depth_jacobian * depth_jacobian, axis=1)
    depth_rhs_slot = jnp.sum(confidence * depth_jacobian * residual, axis=1)
    source_pick = (src_local[:, None] == frame_ids[None, 0:2]).astype(jnp.float32)
    pose_depth = jnp.einsum("sf,sip->fip", source_pick, pose_depth_slot, precision=PRECISE)
    depth_depth = DEPTH_DAMPING + jnp.einsum(
        "sf,sp->fp", source_pick, depth_depth_slot, precision=PRECISE
    )
    depth_rhs = jnp.einsum("sf,sp->fp", source_pick, depth_rhs_slot, precision=PRECISE)
    depth_ratio = pose_depth / depth_depth[:, None, :]
    reduced = pose_pose - jnp.einsum("fip,fjp->ij", depth_ratio, pose_depth, precision=PRECISE)
    reduced_rhs = pose_rhs - jnp.einsum("fip,fp->i", depth_ratio, depth_rhs, precision=PRECISE)
    return (reduced, reduced_rhs, pose_depth, depth_depth, depth_rhs)


def factor_solve(factor_low, rhs_mat):
    lower_part = lax.linalg.triangular_solve(factor_low, rhs_mat, left_side=True, lower=True)
    return lax.linalg.triangular_solve(
        factor_low, lower_part, left_side=True, lower=True, transpose_a=True
    )


def sweep_nodes(blocks, vectors):
    node_total = blocks.shape[0]
    node_ids = jnp.arange(node_total, dtype=jnp.int32)
    same_node = (node_ids[:, None] == node_ids[None, :]).astype(jnp.float32)
    next_node = (node_ids[None, :] == node_ids[:, None] + 1).astype(jnp.float32)
    previous_far = jnp.concatenate(
        [jnp.zeros((1, 12, 12), jnp.float32), blocks[:-1, 12:, 12:]], axis=0
    )
    diag_blocks = blocks[:, :12, :12] + previous_far
    link_blocks = blocks[:, :12, 12:]
    dense = jnp.einsum("nm,nij->nimj", same_node, diag_blocks, precision=PRECISE)
    upper = jnp.einsum("nm,nij->nimj", next_node, link_blocks, precision=PRECISE)
    dense = dense + upper + jnp.transpose(upper, (2, 3, 0, 1))
    system_size = 12 * node_total
    system = dense.reshape(system_size, system_size) + POSE_DAMPING * jnp.eye(
        system_size, dtype=jnp.float32
    )
    previous_rhs = jnp.concatenate([jnp.zeros((1, 12), jnp.float32), vectors[:-1, 12:]], axis=0)
    system_rhs = (vectors[:, :12] + previous_rhs).reshape(system_size)
    factor_low = jnp.linalg.cholesky(system)
    solution = factor_solve(factor_low, system_rhs[:, None])[:, 0]
    return solution.reshape(node_total, 12)


def shards(features, poses, inv_depth, hidden, edges, counts, w_gates, w_cand, w_head):
    slot_count, row_count, col_count, hid_width = hidden.shape
    channels = features.shape[3]
    frame_count = poses.shape[0]
    node_rank = lax.axis_index("edge")
    base_frame = 2 * node_rank
    pix_rank = lax.axis_index("pix")
    total_rows = row_count * lax.axis_size("pix")
    local_pixels = row_count * col_count
    own_whole = lax.all_gather(features, "pix", axis=1, tiled=True)
    next_whole = passed_along(own_whole, "edge", -1)
    nearby = jnp.concatenate([own_whole, next_whole], axis=0)
    nearby = nearby.reshape(4, total_rows * col_count, channels)
    own_flat = features.reshape(2, local_pixels, channels)
    src_local = edges[:, 0] - base_frame
    tgt_local = edges[:, 1] - base_frame
    factor = 2.0 / math.sqrt(channels)
    matched_list = []
    for slot_index in range(slot_count):
        queries = lax.dynamic_index_in_dim(own_flat, src_local[slot_index], 0, keepdims=False)
        targets = lax.dynamic_index_in_dim(nearby, tgt_local[slot_index], 0, keepdims=False)
        matched_list.append(match_rows(queries, targets, factor))
    matched = jnp.stack(matched_list, axis=0).reshape(slot_count, row_count, col_count, channels)
    inputs = jnp.concatenate([hidden, matched], axis=3)
    state_wide = hidden.astype(jnp.float32)
    framed = padded_2(inputs, (("pix", 1),), 1)
    gates = jax.nn.sigmoid(conv_taps(framed, w_gates, row_count, col_count))
    update = gates[..., :hid_width]
    reset_state = (gates[..., hid_width:] * state_wide).astype(jnp.bfloat16)
    reset_framed = padded_2(reset_state, (("pix", 1),), 1)
    second = jnp.concatenate([reset_framed, framed[..., hid_width:]], axis=3)
    candidate = jnp.tanh(conv_taps(second, w_cand, row_count, col_count))
    fresh = ((1.0 - update) * state_wide + update * candidate).astype(jnp.bfloat16)
    live_mask = (lax.broadcasted_iota(jnp.int32, (slot_count,), 0) < counts[0]).astype(jnp.float32)
    hidden_out = jnp.where(live_mask[:, None, None, None] > 0.5, fresh, hidden)
    head_out = jnp.einsum(
        "kc,spc->skp",
        w_head,
        fresh.reshape(slot_count, local_pixels, hid_width),
        preferred_element_type=jnp.float32,
    )
    pair_ids = jnp.arange(2, dtype=jnp.int32)
    source_pick = (src_local[:, None] == pair_ids[None, :]).astype(jnp.float32)
    inv_rho = jnp.dot(source_pick, inv_depth, precision=PRECISE)
    all_ids = jnp.arange(frame_count, dtype=jnp.int32)
    frame_diff = (edges[:, 1:2] == all_ids[None, :]).astype(jnp.float32) - (
        edges[:, 0:1] == all_ids[None, :]
    ).astype(jnp.float32)
    xi_rel = jnp.dot(frame_diff, poses, precision=PRECISE)
    horizontal, vertical = pixel_coords(pix_rank * row_count, row_count, total_rows, col_count)
    reduced_part, rhs_part, pose_depth, depth_depth, depth_rhs = bundle_terms(
        head_out, live_mask, inv_rho, xi_rel, src_local, tgt_local, horizontal, vertical
    )
    reduced, reduced_rhs = lax.psum((reduced_part, rhs_part), "pix")
    blocks, vectors = (
        lax.all_gather(reduced[None], "edge", axis=0, tiled=True),
        lax.all_gather(reduced_rhs[None], "edge", axis=0, tiled=True),
    )
    values = sweep_nodes(blocks, vectors)
    node_total = values.shape[0]
    node_pose = lax.dynamic_index_in_dim(values, node_rank, 0, keepdims=False)
    after_index = jnp.minimum(node_rank + 1, node_total - 1)
    next_pose = lax.dynamic_index_in_dim(values, after_index, 0, keepdims=False) * (
        node_rank + 1 < node_total
    ).astype(jnp.float32)
    pose_update = node_pose.reshape(2, 6)
    pose_pair = jnp.concatenate([node_pose, next_pose], axis=0)
    depth_update = (
        depth_rhs - jnp.einsum("fip,i->fp", pose_depth, pose_pair, precision=PRECISE)
    ) / depth_depth
    return (hidden_out, pose_update, depth_update)


def solution(mesh):
    placed = (
        P("edge", "pix", None, None),
        P(),
        P("edge", "pix"),
        P("edge", "pix", None, None),
        P("edge", None),
        P("edge"),
        P(),
        P(),
        P(),
    )
    return jax.shard_map(
        shards,
        mesh=mesh,
        in_specs=placed,
        out_specs=(P("edge", "pix", None, None), P("edge", None), P("edge", "pix")),
        check_vma=False,
    )
```

profile of v0, /device:TPU:1, one launch (start us, length us, event | category | flops | bytes accessed | tf_op | source)
XLA Modules:
  0.0 581.9 jit_solution(17546545287537749910)
XLA Ops:
  22.5 20.2 %all-gather.3.cloned.1.call-done = bf16[2,48,64,128]{3,2,1,0:T(8,128)(2,1)} async-done(((bf16[2,12,64,128]{3,2,1,0:T(8,128)(2,1)}), bf16[2,48,64,128]{3,2,1,0:T(8,128)(2,1)}) %all-gather.3.cloned.1.call-update) | async-done | bytes 1572880 | tf_op jit(solution)/shard_map/all_gather | solution.py:174
  51.2 13.6 %collective-permute-done = bf16[2,48,64,128]{3,2,1,0:T(8,128)(2,1)S(1)} collective-permute-done((bf16[2,48,64,128]{3,2,1,0:T(8,128)(2,1)}, bf16[2,48,64,128]{3,2,1,0:T(8,128)(2,1)S(1)}, u32[]{:S(2)}, u32[]{:S(2)}) %collective-permute-start) | collective-permute-done | bytes 1572896 | tf_op jit(solution)/shard_map/ppermute | solution.py:15
  103.2 4.9 add_divide_fusion
  109.7 4.4 collective-permute-start.3
  126.7 13.3 %all-reduce.5 = (f32[1,24,24]{2,1,0:T(8,128)S(1)}, f32[1,24]{1,0:T(1,128)S(1)}) all-reduce(f32[1,24,24]{2,1,0:T(8,128)S(1)} %fusion.97, f32[1,24]{1,0:T(1,128)S(1)} %fusion.106), channel_id=1, replica_groups=mesh['edge'=64,'pix'=4] {'pix'}, use_global_device_ids=true, to_apply=%region_9.10 | all-reduce | flops 600 | bytes 4800 | tf_op jit(solution)/shard_map/psum | solution.py:218
  139.9 58.5 %all_gather.10 = f32[64,24,24]{2,1,0:T(8,128)S(1)} all-gather(f32[1,24,24]{2,1,0:T(8,128)S(1)} %get-tuple-element.36), channel_id=1, replica_groups=mesh['edge'=64,'pix'=4] {'edge'}, dimensions={0}, use_global_device_ids=true | all-gather | bytes 149760 | tf_op jit(solution)/shard_map/all_gather | solution.py:220
  200.0 12.3 %fusion = f32[64,12,64,12]{1,0,3,2:T(8,128)} fusion(f32[64,64]{0,1:T(8,128)S(1)} %get-tuple-element.125, f32[64,12,12]{1,0,2:T(8,128)S(1)} %copy.62, f32[64,64]{0,1:T(8,128)S(1)} %get-tuple-element.124, f32[64,12,12]{1,0,2:T(8,128)S(1)} %copy.61), kind=kLoop, calls=%fused_computation.4 | loop fusion | flops 1769472 | bytes 2465792 | tf_op jit(solution)/shard_map/add | solution.py:153
  212.3 33.5 %copy.63 = f32[64,12,64,12]{3,2,1,0:T(8,128)} copy(f32[64,12,64,12]{1,0,3,2:T(8,128)} %fusion) | data formatting | bytes 4718592 | tf_op jit(solution)/shard_map/add | solution.py:153
  245.9 18.1 %fusion.1 = f32[64,12,64,12]{3,2,1,0:T(8,128)} fusion(f32[64,12,64,12]{3,2,1,0:T(8,128)} %copy.63, f32[64,64]{0,1:T(8,128)S(1)} %get-tuple-element.125, f32[64,12,12]{1,0,2:T(8,128)S(1)} %copy.62), kind=kLoop, calls=%fused_computation.5 | loop fusion | flops 1179648 | bytes 4771840 | tf_op jit(solution)/shard_map/add | solution.py:153
  264.0 22.7 %reshape.435 = f32[768,768]{1,0:T(8,128)} reshape(f32[64,12,64,12]{3,2,1,0:T(8,128)} %fusion.1) | data formatting | bytes 4718592 | tf_op jit(solution)/shard_map/reshape | solution.py:155
  297.0 11.7 %cholesky.164 = f32[128,128]{1,0:T(8,128)S(1)} custom-call(f32[128,128]{1,0:T(8,128)S(1)} %cholesky.421), custom_call_target="Cholesky" | custom-call | tf_op jit(solution)/shard_map/jit(cholesky)/cholesky | solution.py:160
  308.9 9.8 %custom-call.48 = f32[1,128,128]{1,2,0:T(8,128)S(1)} custom-call(f32[1,128,128]{2,1,0:T(8,128)S(1)} %get-tuple-element.60), custom_call_target="InvertDiagBlocksLowerTriangular" | custom-call | tf_op jit(solution)/shard_map/jit(cholesky)/cholesky | solution.py:160
  321.7 11.7 %cholesky.187 = f32[128,128]{1,0:T(8,128)S(1)} custom-call(f32[128,128]{1,0:T(8,128)S(1)} %cholesky.425), custom_call_target="Cholesky" | custom-call | tf_op jit(solution)/shard_map/jit(cholesky)/cholesky | solution.py:160
  333.5 10.2 %custom-call.49 = f32[1,128,128]{1,2,0:T(8,128)S(1)} custom-call(f32[1,128,128]{2,1,0:T(8,128)S(1)} %get-tuple-element.58), custom_call_target="InvertDiagBlocksLowerTriangular" | custom-call | tf_op jit(solution)/shard_map/jit(cholesky)/cholesky | solution.py:160
  346.3 11.7 %cholesky.352 = f32[128,128]{1,0:T(8,128)S(1)} custom-call(f32[128,128]{1,0:T(8,128)S(1)} %cholesky.430), custom_call_target="Cholesky" | custom-call | tf_op jit(solution)/shard_map/jit(cholesky)/cholesky | solution.py:160
  358.2 9.8 %custom-call.50 = f32[1,128,128]{1,2,0:T(8,128)S(1)} custom-call(f32[1,128,128]{2,1,0:T(8,128)S(1)} %get-tuple-element.56), custom_call_target="InvertDiagBlocksLowerTriangular" | custom-call | tf_op jit(solution)/shard_map/jit(cholesky)/cholesky | solution.py:160
  370.5 11.9 %cholesky.371 = f32[128,128]{1,0:T(8,128)S(1)} custom-call(f32[128,128]{1,0:T(8,128)S(1)} %cholesky.435), custom_call_target="Cholesky" | custom-call | tf_op jit(solution)/shard_map/jit(cholesky)/cholesky | solution.py:160
  382.6 9.8 %custom-call.51 = f32[1,128,128]{1,2,0:T(8,128)S(1)} custom-call(f32[1,128,128]{2,1,0:T(8,128)S(1)} %get-tuple-element.54), custom_call_target="InvertDiagBlocksLowerTriangular" | custom-call | tf_op jit(solution)/shard_map/jit(cholesky)/cholesky | solution.py:160
  394.6 11.7 %cholesky.390 = f32[128,128]{1,0:T(8,128)S(1)} custom-call(f32[128,128]{1,0:T(8,128)S(1)} %cholesky.440), custom_call_target="Cholesky" | custom-call | tf_op jit(solution)/shard_map/jit(cholesky)/cholesky | solution.py:160
  406.5 9.8 %custom-call.52 = f32[1,128,128]{1,2,0:T(8,128)S(1)} custom-call(f32[1,128,128]{2,1,0:T(8,128)S(1)} %get-tuple-element.52), custom_call_target="InvertDiagBlocksLowerTriangular" | custom-call | tf_op jit(solution)/shard_map/jit(cholesky)/cholesky | solution.py:160
  418.4 11.7 %cholesky.408 = f32[128,128]{1,0:T(8,128)S(1)} custom-call(f32[128,128]{1,0:T(8,128)S(1)} %convolution_subtract_fusion.4), custom_call_target="Cholesky" | custom-call | tf_op jit(solution)/shard_map/jit(cholesky)/cholesky | solution.py:160
  434.2 37.7 %all-gather = f32[64,1,24]{2,1,0:T(1,128)S(1)} all-gather(f32[1,1,24]{2,1,0:T(1,128)S(1)} %bitcast.562), channel_id=1, replica_groups=mesh['edge'=64,'pix'=4] {'edge'}, dimensions={0}, use_global_device_ids=true | all-gather | bytes 6240 | tf_op jit(solution)/shard_map/all_gather | solution.py:221
  477.5 21.6 %while.1 = (s32[]{:T(128)}, f32[768,768]{0,1:T(8,128)}, s32[6,2]{0,1:T(2,128)S(1)}, f32[6,128,128]{2,1,0:T(8,128)}, s32[]{:T(128)}) while((s32[]{:T(128)}, f32[768,768]{0,1:T(8,128)}, s32[6,2]{0,1:T(2,128)S(1)}, f32[6,128,128]{2,1,0:T(8,128)}, s32[]{:T(128)}) %tuple.82), condition=%wide.while_cond, body=%wide.while_body.sunk | while | flops 2 | bytes 393329 | solution.py:136
  499.1 59.8 %custom-call.53 = f32[6,128,128]{1,2,0:T(8,128)S(1)} custom-call(f32[6,128,128]{2,1,0:T(8,128)} %get-tuple-element.10), custom_call_target="InvertDiagBlocksLowerTriangular" | custom-call | tf_op jit(solution)/shard_map/triangular_solve | solution.py:136
  (231 shorter events, 128.4 us)
Async XLA Ops:
  7.2 15.0 %copy-start = (f32[2,768]{1,0:T(2,128)S(1)}, f32[2,768]{1,0:T(2,128)}, u32[]{:S(2)}) copy-start(f32[2,768]{1,0:T(2,128)} %param.11) | copy-start | bytes 18436
  7.2 35.5 %all-gather.3.cloned.1.call-start = ((), (), s32[]{:S(2)}) async-start(), calls=%async_computation | async-start | bytes 1966080 | tf_op jit(solution)/shard_map/all_gather | solution.py:174
  42.7 22.0 %collective-permute-start = (bf16[2,48,64,128]{3,2,1,0:T(8,128)(2,1)}, bf16[2,48,64,128]{3,2,1,0:T(8,128)(2,1)S(1)}, u32[]{:S(2)}, u32[]{:S(2)}) collective-permute-start(bf16[2,48,64,128]{3,2,1,0:T(8,128)(2,1)} %all-gather.3.cloned.1.call-done), channel_id=1, source_target_pairs={{4,0},{8,4},{12,8},{16,12},{20,16},{24,20},{28,24},{32,28},{36,32}... | collective-permute-start | bytes 4718600 | tf_op jit(solution)/shard_map/ppermute | solution.py:15
  51.2 15.3 %copy-start.4 = (bf16[2,12,64,128]{3,2,1,0:T(8,128)(2,1)S(1)}, bf16[2,12,64,128]{3,2,1,0:T(8,128)(2,1)}, u32[]{:S(2)}) copy-start(bf16[2,12,64,128]{3,2,1,0:T(8,128)(2,1)} %param.9) | copy-start | bytes 1179652
  85.7 2.1 copy-start.2
  85.7 7.5 %copy-start.5 = (bf16[9,256,256]{2,1,0:T(8,128)(2,1)S(1)}, bf16[9,256,256]{2,1,0:T(8,128)(2,1)}, u32[]{:S(2)}) copy-start(bf16[9,256,256]{2,1,0:T(8,128)(2,1)} %param.15) | copy-start | bytes 3538948
  87.9 7.6 %collective-permute-start.2 = (bf16[4,1,64,256]{3,2,1,0:T(8,128)(2,1)S(1)}, bf16[4,1,64,256]{3,2,1,0:T(8,128)(2,1)S(1)}, u32[]{:S(2)}, u32[]{:S(2)}) collective-permute-start(bf16[4,1,64,256]{3,2,1,0:T(8,128)(2,1)S(1)} %get-tuple-element.45), channel_id=1, source_target_pairs={{1,0},{2,1},{3,2},{5,4},{6,5},{7,6},{9,8},{10,9},{11,10},{13,12},{... | collective-permute-start | bytes 393224 | tf_op jit(solution)/shard_map/ppermute | solution.py:28
  89.2 6.3 %collective-permute-start.1 = (bf16[4,1,64,256]{3,2,1,0:T(8,128)(2,1)S(1)}, bf16[4,1,64,256]{3,2,1,0:T(8,128)(2,1)S(1)}, u32[]{:S(2)}, u32[]{:S(2)}) collective-permute-start(bf16[4,1,64,256]{3,2,1,0:T(8,128)(2,1)S(1)} %get-tuple-element.44), channel_id=1, source_target_pairs={{0,1},{1,2},{2,3},{4,5},{5,6},{6,7},{8,9},{9,10},{10,11},{12,13},{... | collective-permute-start | bytes 393224 | tf_op jit(solution)/shard_map/ppermute | solution.py:26
  108.4 6.0 %collective-permute-start.4 = (bf16[4,1,64,128]{3,2,1,0:T(8,128)(2,1)S(1)}, bf16[4,1,64,128]{3,2,1,0:T(8,128)(2,1)S(1)}, u32[]{:S(2)}, u32[]{:S(2)}) collective-permute-start(bf16[4,1,64,128]{3,2,1,0:T(8,128)(2,1)S(1)} %get-tuple-element.49), channel_id=1, source_target_pairs={{1,0},{2,1},{3,2},{5,4},{6,5},{7,6},{9,8},{10,9},{11,10},{13,12},{... | collective-permute-start | bytes 196616 | tf_op jit(solution)/shard_map/ppermute | solution.py:28
  109.7 5.4 collective-permute-start.3
  114.2 1.2 copy-start.6
  120.0 2.3 copy-start.7
  295.6 1.4 copy-start.3
  477.5 97.4 %copy-start.1 = (f32[2,768]{1,0:T(2,128)S(1)}, f32[2,768]{1,0:T(2,128)}, u32[]{:S(2)}) copy-start(f32[2,768]{1,0:T(2,128)} %param.11) | copy-start | bytes 18436
Sparse Core Ops, SparseCore 0:
  9.8 32.8 all-gather.2
where the time goes:
time: 588 us; the launch traced here: 582 us
  other arithmetic  232 us (39%)
  blocking collectives  109 us (19%)
  local copies, waits for them, and re-layouts  89.6 us (15%)
  matrix products  66.9 us (11%)
  waiting for transfers between devices  35.2 us (6%)
  between operations  34.7 us (6%)
  starting transfers between devices  13.6 us (2%)
    another operation x23, other arithmetic, sweep_nodes(): factor_low = jnp.linalg.cholesky(system)  124 us
    another operation x4, other arithmetic, factor_solve(): lax.linalg.triangular_solve(factor_low, lower_part, left_side=True, lower...  61.4 us
    all_gather x1, blocking collectives, shards(): lax.all_gather(reduced[None], 'edge', axis=0, tiled=True)  58.5 us
    all_gather x1, blocking collectives, shards(): lax.all_gather(reduced_rhs[None], 'edge', axis=0, tiled=True)  37.7 us
    add x1, local copies, waits for them, and re-layouts, sweep_nodes(): dense = dense + upper + jnp.transpose(upper, (2, 3, 0, 1))  33.5 us
    add x2, other arithmetic, sweep_nodes(): dense = dense + upper + jnp.transpose(upper, (2, 3, 0, 1))  30.4 us
    reshape x2, local copies, waits for them, and re-layouts, sweep_nodes(): dense.reshape(system_size, system_size)  24.7 us
    another operation x30, local copies, waits for them, and re-layouts  21.5 us
  transfers between devices with their start and end apart: 6, of which 3 were waited for; matrix products, arithmetic and copies ran while one was open for 1% of the time, Pallas kernels for 0%

commit v1 on v0

--- a/solution.py
+++ b/solution.py
@@ -171,7 +171,25 @@
     pix_rank = lax.axis_index("pix")
     total_rows = row_count * lax.axis_size("pix")
     local_pixels = row_count * col_count
-    own_whole = lax.all_gather(features, "pix", axis=1, tiled=True)
+    peers, index, rows = (lax.axis_size("pix"), lax.axis_index("pix"), features.shape[1])
+    right = [(i_2, (i_2 + 1) % peers) for i_2 in range(peers)]
+    downward = [(i_2, (i_2 - 1) % peers) for i_2 in range(peers)]
+    own_whole = jnp.zeros(
+        (*features.shape[:1], peers * rows, *features.shape[1 + 1 :]), features.dtype
+    )
+    own_whole = lax.dynamic_update_slice_in_dim(own_whole, features, index * rows, axis=1)
+    from_left = from_right = features
+    half = peers // 2
+    for step in range(1, half + 1):
+        from_left = lax.ppermute(from_left, "pix", right)
+        own_whole = lax.dynamic_update_slice_in_dim(
+            own_whole, from_left, (index - step) % peers * rows, axis=1
+        )
+        if step < peers - half:
+            from_right = lax.ppermute(from_right, "pix", downward)
+            own_whole = lax.dynamic_update_slice_in_dim(
+                own_whole, from_right, (index + step) % peers * rows, axis=1
+            )
     next_whole = passed_along(own_whole, "edge", -1)
     nearby = jnp.concatenate([own_whole, next_whole], axis=0)
     nearby = nearby.reshape(4, total_rows * col_count, channels)

time: 588 us -> 568 us (0.966)
  waiting for transfers between devices: 35.2 us -> 16 us
  between operations: 34.7 us -> 21.4 us
  starting transfers between devices: 13.6 us -> 20.4 us
    all_gather x1 -> x0, waiting for transfers between devices: 20.2 us -> none  [shards(): own_whole = lax.all_gather(features, 'pix', axis=1, tiled=True)]
  transfers between devices with their start and end apart: 6 -> 8, of which waited for: 3 -> 3; matrix products, arithmetic and copies ran while one was open for 1% -> 2% of each run, Pallas kernels for 0% -> 0%
where the time goes in v1:
time: 568 us; the launch traced here: 561 us
  other arithmetic  234 us (41%)
  blocking collectives  111 us (20%)
  local copies, waits for them, and re-layouts  90.3 us (16%)
  matrix products  66.9 us (12%)
  between operations  21.4 us (4%)
  starting transfers between devices  20.4 us (4%)
  waiting for transfers between devices  16 us (3%)
    another operation x23, other arithmetic, sweep_nodes(): factor_low = jnp.linalg.cholesky(system)  124 us
    another operation x4, other arithmetic, factor_solve(): lax.linalg.triangular_solve(factor_low, lower_part, left_side=True, lower...  61.9 us
    all_gather x1, blocking collectives, shards(): lax.all_gather(reduced[None], 'edge', axis=0, tiled=True)  59.8 us
    all_gather x1, blocking collectives, shards(): lax.all_gather(reduced_rhs[None], 'edge', axis=0, tiled=True)  37.3 us
    add x1, local copies, waits for them, and re-layouts, sweep_nodes(): dense = dense + upper + jnp.transpose(upper, (2, 3, 0, 1))  33.5 us
    add x2, other arithmetic, sweep_nodes(): dense = dense + upper + jnp.transpose(upper, (2, 3, 0, 1))  30.4 us
    reshape x2, local copies, waits for them, and re-layouts, sweep_nodes(): dense.reshape(system_size, system_size)  24.7 us
    another operation x30, local copies, waits for them, and re-layouts  21.5 us
  transfers between devices with their start and end apart: 8, of which 3 were waited for; matrix products, arithmetic and copies ran while one was open for 2% of the time, Pallas kernels for 0%

profile of v1, /device:TPU:1, one launch (start us, length us, event | category | flops | bytes accessed | tf_op | source)
XLA Modules:
  0.0 560.6 jit_solution(17116668057972166169)
XLA Ops:
  24.4 4.0 collective-permute-start.3
  35.9 12.2 %collective-permute-done.3 = bf16[2,48,64,128]{3,2,1,0:T(8,128)(2,1)} collective-permute-done((bf16[2,48,64,128]{3,2,1,0:T(8,128)(2,1)S(1)}, bf16[2,48,64,128]{3,2,1,0:T(8,128)(2,1)}, u32[]{:S(2)}, u32[]{:S(2)}) %collective-permute-start.3) | collective-permute-done | bytes 1572896 | tf_op jit(solution)/shard_map/ppermute | solution.py:15
  86.6 4.9 add_divide_fusion
  93.0 4.4 collective-permute-start.6
  110.1 14.3 %all-reduce.5 = (f32[1,24,24]{2,1,0:T(8,128)S(1)}, f32[1,24]{1,0:T(1,128)S(1)}) all-reduce(f32[1,24,24]{2,1,0:T(8,128)S(1)} %fusion.97, f32[1,24]{1,0:T(1,128)S(1)} %fusion.106), channel_id=1, replica_groups=mesh['edge'=64,'pix'=4] {'pix'}, use_global_device_ids=true, to_apply=%region_9.10 | all-reduce | flops 600 | bytes 4800 | tf_op jit(solution)/shard_map/psum | solution.py:236
  124.4 59.8 %all_gather.6 = f32[64,24,24]{2,1,0:T(8,128)S(1)} all-gather(f32[1,24,24]{2,1,0:T(8,128)S(1)} %get-tuple-element.36), channel_id=1, replica_groups=mesh['edge'=64,'pix'=4] {'edge'}, dimensions={0}, use_global_device_ids=true | all-gather | bytes 149760 | tf_op jit(solution)/shard_map/all_gather | solution.py:238
  185.9 12.3 %fusion = f32[64,12,64,12]{1,0,3,2:T(8,128)} fusion(f32[64,64]{0,1:T(8,128)S(1)} %get-tuple-element.125, f32[64,12,12]{1,0,2:T(8,128)S(1)} %copy.62, f32[64,64]{0,1:T(8,128)S(1)} %get-tuple-element.124, f32[64,12,12]{1,0,2:T(8,128)S(1)} %copy.61), kind=kLoop, calls=%fused_computation.4 | loop fusion | flops 1769472 | bytes 2465792 | tf_op jit(solution)/shard_map/add | solution.py:153
  198.2 33.5 %copy.63 = f32[64,12,64,12]{3,2,1,0:T(8,128)} copy(f32[64,12,64,12]{1,0,3,2:T(8,128)} %fusion) | data formatting | bytes 4718592 | tf_op jit(solution)/shard_map/add | solution.py:153
  231.7 18.1 %fusion.1 = f32[64,12,64,12]{3,2,1,0:T(8,128)} fusion(f32[64,12,64,12]{3,2,1,0:T(8,128)} %copy.63, f32[64,64]{0,1:T(8,128)S(1)} %get-tuple-element.125, f32[64,12,12]{1,0,2:T(8,128)S(1)} %copy.62), kind=kLoop, calls=%fused_computation.5 | loop fusion | flops 1179648 | bytes 4771840 | tf_op jit(solution)/shard_map/add | solution.py:153
  249.8 22.7 %reshape.435 = f32[768,768]{1,0:T(8,128)} reshape(f32[64,12,64,12]{3,2,1,0:T(8,128)} %fusion.1) | data formatting | bytes 4718592 | tf_op jit(solution)/shard_map/reshape | solution.py:155
  282.9 11.7 %cholesky.164 = f32[128,128]{1,0:T(8,128)S(1)} custom-call(f32[128,128]{1,0:T(8,128)S(1)} %cholesky.421), custom_call_target="Cholesky" | custom-call | tf_op jit(solution)/shard_map/jit(cholesky)/cholesky | solution.py:160
  294.7 9.8 %custom-call.48 = f32[1,128,128]{1,2,0:T(8,128)S(1)} custom-call(f32[1,128,128]{2,1,0:T(8,128)S(1)} %get-tuple-element.60), custom_call_target="InvertDiagBlocksLowerTriangular" | custom-call | tf_op jit(solution)/shard_map/jit(cholesky)/cholesky | solution.py:160
  307.5 11.7 %cholesky.187 = f32[128,128]{1,0:T(8,128)S(1)} custom-call(f32[128,128]{1,0:T(8,128)S(1)} %cholesky.425), custom_call_target="Cholesky" | custom-call | tf_op jit(solution)/shard_map/jit(cholesky)/cholesky | solution.py:160
  319.4 10.2 %custom-call.49 = f32[1,128,128]{1,2,0:T(8,128)S(1)} custom-call(f32[1,128,128]{2,1,0:T(8,128)S(1)} %get-tuple-element.58), custom_call_target="InvertDiagBlocksLowerTriangular" | custom-call | tf_op jit(solution)/shard_map/jit(cholesky)/cholesky | solution.py:160
  332.2 11.7 %cholesky.352 = f32[128,128]{1,0:T(8,128)S(1)} custom-call(f32[128,128]{1,0:T(8,128)S(1)} %cholesky.430), custom_call_target="Cholesky" | custom-call | tf_op jit(solution)/shard_map/jit(cholesky)/cholesky | solution.py:160
  344.1 9.8 %custom-call.50 = f32[1,128,128]{1,2,0:T(8,128)S(1)} custom-call(f32[1,128,128]{2,1,0:T(8,128)S(1)} %get-tuple-element.56), custom_call_target="InvertDiagBlocksLowerTriangular" | custom-call | tf_op jit(solution)/shard_map/jit(cholesky)/cholesky | solution.py:160
  356.4 11.9 %cholesky.371 = f32[128,128]{1,0:T(8,128)S(1)} custom-call(f32[128,128]{1,0:T(8,128)S(1)} %cholesky.435), custom_call_target="Cholesky" | custom-call | tf_op jit(solution)/shard_map/jit(cholesky)/cholesky | solution.py:160
  368.4 9.8 %custom-call.51 = f32[1,128,128]{1,2,0:T(8,128)S(1)} custom-call(f32[1,128,128]{2,1,0:T(8,128)S(1)} %get-tuple-element.54), custom_call_target="InvertDiagBlocksLowerTriangular" | custom-call | tf_op jit(solution)/shard_map/jit(cholesky)/cholesky | solution.py:160
  380.5 11.7 %cholesky.390 = f32[128,128]{1,0:T(8,128)S(1)} custom-call(f32[128,128]{1,0:T(8,128)S(1)} %cholesky.440), custom_call_target="Cholesky" | custom-call | tf_op jit(solution)/shard_map/jit(cholesky)/cholesky | solution.py:160
  392.3 9.8 %custom-call.52 = f32[1,128,128]{1,2,0:T(8,128)S(1)} custom-call(f32[1,128,128]{2,1,0:T(8,128)S(1)} %get-tuple-element.52), custom_call_target="InvertDiagBlocksLowerTriangular" | custom-call | tf_op jit(solution)/shard_map/jit(cholesky)/cholesky | solution.py:160
  404.2 11.7 %cholesky.408 = f32[128,128]{1,0:T(8,128)S(1)} custom-call(f32[128,128]{1,0:T(8,128)S(1)} %convolution_subtract_fusion.4), custom_call_target="Cholesky" | custom-call | tf_op jit(solution)/shard_map/jit(cholesky)/cholesky | solution.py:160
  420.0 37.3 %all-gather = f32[64,1,24]{2,1,0:T(1,128)S(1)} all-gather(f32[1,1,24]{2,1,0:T(1,128)S(1)} %bitcast.562), channel_id=1, replica_groups=mesh['edge'=64,'pix'=4] {'edge'}, dimensions={0}, use_global_device_ids=true | all-gather | bytes 6240 | tf_op jit(solution)/shard_map/all_gather | solution.py:239
  463.0 21.6 %while.1 = (s32[]{:T(128)}, f32[768,768]{0,1:T(8,128)}, s32[6,2]{0,1:T(2,128)S(1)}, f32[6,128,128]{2,1,0:T(8,128)}, s32[]{:T(128)}) while((s32[]{:T(128)}, f32[768,768]{0,1:T(8,128)}, s32[6,2]{0,1:T(2,128)S(1)}, f32[6,128,128]{2,1,0:T(8,128)}, s32[]{:T(128)}) %tuple.82), condition=%wide.while_cond, body=%wide.while_body.sunk | while | flops 2 | bytes 393329 | solution.py:136
  484.6 59.8 %custom-call.53 = f32[6,128,128]{1,2,0:T(8,128)S(1)} custom-call(f32[6,128,128]{2,1,0:T(8,128)} %get-tuple-element.10), custom_call_target="InvertDiagBlocksLowerTriangular" | custom-call | tf_op jit(solution)/shard_map/triangular_solve | solution.py:136
  (249 shorter events, 135.8 us)
Async XLA Ops:
  0.6 4.3 copy-start
  0.6 23.4 %copy-start.4 = (bf16[2,12,64,128]{3,2,1,0:T(8,128)(2,1)S(1)}, bf16[2,12,64,128]{3,2,1,0:T(8,128)(2,1)}, u32[]{:S(2)}) copy-start(bf16[2,12,64,128]{3,2,1,0:T(8,128)(2,1)} %param.9) | copy-start | bytes 1179652
  0.7 10.1 %collective-permute-start = (bf16[2,12,64,128]{3,2,1,0:T(8,128)(2,1)}, bf16[2,12,64,128]{3,2,1,0:T(8,128)(2,1)S(1)}, u32[]{:S(2)}, u32[]{:S(2)}) collective-permute-start(bf16[2,12,64,128]{3,2,1,0:T(8,128)(2,1)} %param.9), channel_id=1, source_target_pairs={{0,1},{1,2},{2,3},{3,0},{4,5},{5,6},{6,7},{7,4},{8,9},{9,10},{10,1... | collective-permute-start | bytes 1179656 | tf_op jit(solution)/shard_map/ppermute | solution.py:184
  2.8 21.4 %collective-permute-start.1 = (bf16[2,12,64,128]{3,2,1,0:T(8,128)(2,1)}, bf16[2,12,64,128]{3,2,1,0:T(8,128)(2,1)S(1)}, u32[]{:S(2)}, u32[]{:S(2)}) collective-permute-start(bf16[2,12,64,128]{3,2,1,0:T(8,128)(2,1)} %param.9), channel_id=1, source_target_pairs={{0,3},{1,0},{2,1},{3,2},{4,7},{5,4},{6,5},{7,6},{8,11},{9,8},{10,9... | collective-permute-start | bytes 1179656 | tf_op jit(solution)/shard_map/ppermute | solution.py:189
  4.9 24.3 %copy-start.8 = (s32[4]{0:T(128)}, s32[4]{0:T(128)S(1)}, u32[]{:S(2)}) copy-start(s32[4]{0:T(128)S(1)} %get-tuple-element.78) | copy-start | bytes 52
  10.8 13.5 %collective-permute-start.2 = (bf16[2,12,64,128]{3,2,1,0:T(8,128)(2,1)S(1)}, bf16[2,12,64,128]{3,2,1,0:T(8,128)(2,1)S(1)}, u32[]{:S(2)}, u32[]{:S(2)}) collective-permute-start(bf16[2,12,64,128]{3,2,1,0:T(8,128)(2,1)S(1)} %collective-permute-done), channel_id=1, source_target_pairs={{0,1},{1,2},{2,3},{3,0},{4,5},{5,6},{6,7},{7,4},{8,9},{9,10},{10,1... | collective-permute-start | bytes 1179656 | tf_op jit(solution)/shard_map/ppermute | solution.py:184
  24.4 23.7 %collective-permute-start.3 = (bf16[2,48,64,128]{3,2,1,0:T(8,128)(2,1)S(1)}, bf16[2,48,64,128]{3,2,1,0:T(8,128)(2,1)}, u32[]{:S(2)}, u32[]{:S(2)}) collective-permute-start(bf16[2,48,64,128]{3,2,1,0:T(8,128)(2,1)S(1)} %constant_dynamic-update-slice_fusion.28), channel_id=1, source_target_pairs={{4,0},{8,4},{12,8},{16,12},{20,16},{24,20},{28,24},{32,28},{36,32}... | collective-permute-start | bytes 4718600 | tf_op jit(solution)/shard_map/ppermute | solution.py:15
  69.0 2.1 copy-start.2
  69.0 7.5 %copy-start.5 = (bf16[9,256,256]{2,1,0:T(8,128)(2,1)S(1)}, bf16[9,256,256]{2,1,0:T(8,128)(2,1)}, u32[]{:S(2)}) copy-start(bf16[9,256,256]{2,1,0:T(8,128)(2,1)} %param.15) | copy-start | bytes 3538948
  71.2 7.6 %collective-permute-start.5 = (bf16[4,1,64,256]{3,2,1,0:T(8,128)(2,1)S(1)}, bf16[4,1,64,256]{3,2,1,0:T(8,128)(2,1)S(1)}, u32[]{:S(2)}, u32[]{:S(2)}) collective-permute-start(bf16[4,1,64,256]{3,2,1,0:T(8,128)(2,1)S(1)} %get-tuple-element.45), channel_id=1, source_target_pairs={{1,0},{2,1},{3,2},{5,4},{6,5},{7,6},{9,8},{10,9},{11,10},{13,12},{... | collective-permute-start | bytes 393224 | tf_op jit(solution)/shard_map/ppermute | solution.py:28
  72.5 6.3 %collective-permute-start.4 = (bf16[4,1,64,256]{3,2,1,0:T(8,128)(2,1)S(1)}, bf16[4,1,64,256]{3,2,1,0:T(8,128)(2,1)S(1)}, u32[]{:S(2)}, u32[]{:S(2)}) collective-permute-start(bf16[4,1,64,256]{3,2,1,0:T(8,128)(2,1)S(1)} %get-tuple-element.44), channel_id=1, source_target_pairs={{0,1},{1,2},{2,3},{4,5},{5,6},{6,7},{8,9},{9,10},{10,11},{12,13},{... | collective-permute-start | bytes 393224 | tf_op jit(solution)/shard_map/ppermute | solution.py:26
  91.7 6.0 %collective-permute-start.7 = (bf16[4,1,64,128]{3,2,1,0:T(8,128)(2,1)S(1)}, bf16[4,1,64,128]{3,2,1,0:T(8,128)(2,1)S(1)}, u32[]{:S(2)}, u32[]{:S(2)}) collective-permute-start(bf16[4,1,64,128]{3,2,1,0:T(8,128)(2,1)S(1)} %get-tuple-element.49), channel_id=1, source_target_pairs={{1,0},{2,1},{3,2},{5,4},{6,5},{7,6},{9,8},{10,9},{11,10},{13,12},{... | collective-permute-start | bytes 196616 | tf_op jit(solution)/shard_map/ppermute | solution.py:28
  93.0 5.4 collective-permute-start.6
  97.5 1.2 copy-start.6
  102.8 0.7 copy-start.11
  103.4 2.3 copy-start.10
  103.4 2.6 copy-start.7
  103.4 2.8 copy-start.9
  281.5 1.4 copy-start.3
  461.3 1.6 copy-start.12
  463.0 97.4 %copy-start.1 = (f32[2,768]{1,0:T(2,128)S(1)}, f32[2,768]{1,0:T(2,128)}, u32[]{:S(2)}) copy-start(f32[2,768]{1,0:T(2,128)} %param.11) | copy-start | bytes 18436
